TPU v7x, 32 devices: a whole 2x2x4 slice. The times are simulated.
32 devices in a mesh: phys: 4 (over y, x), row: 2 (over core), col: 4 (over z).
Axes of the slice: x: 2, y: 2, z: 4, core: 2. Of those that a mesh axis runs over, the one named last changes fastest.
Arguments:
- rho_sites: bfloat16 [1, 16, 2048, 2048], P(None, 'phys', 'row', 'col'), may hold values from -0.0625 to 0.0625
- sigma_sites: bfloat16 [1, 16, 2048, 2048], P(None, 'phys', 'row', 'col'), may hold values from -0.0625 to 0.0625
- environment: float32 [2048, 2048], P('row', 'col'), may hold values from -6 to 6
Outputs:
- new_environment: float32 [2048, 2048], P('row', 'col')
All inputs are finite; a program needn't handle non-finite values.
Results may differ from a plain program's by a relative error of at most 0.004.
Values may be sent and summed in bfloat16 or wider, within the bound.
A program may use at most 128 MiB of HBM per device.

v0:
```python
import jax
import jax.numpy as jnp
from jax import lax
from jax.sharding import PartitionSpec as P


def per_device(rho_sites, sigma_sites, environment):
    env = environment
    rho_block = rho_sites[0]
    sigma_block = sigma_sites[0]
    env_b = env.astype(jnp.bfloat16)
    env_whole = lax.all_gather(env_b, "col", axis=1, tiled=True)
    half = jnp.einsum(
        "ik,pkl->pil",
        env_whole,
        lax.all_gather(sigma_block, "row", axis=1, tiled=True),
        preferred_element_type=jnp.float32,
    ).astype(jnp.bfloat16)
    partial_env = jnp.einsum(
        "pij,pil->jl",
        lax.all_gather(rho_block, "col", axis=2, tiled=True),
        half,
        preferred_element_type=jnp.float32,
    )
    row_part = lax.psum_scatter(partial_env, "row", scatter_dimension=0, tiled=True)
    env = lax.psum(row_part, "phys")
    return env


def solution(mesh):
    placed = (P(None, "phys", "row", "col"), P(None, "phys", "row", "col"), P("row", "col"))
    return jax.shard_map(
        per_device, mesh=mesh, in_specs=placed, out_specs=P("row", "col"), check_vma=False
    )
```

profile of v0, /device:TPU:26, one launch (start us, length us, event | category | flops | bytes accessed | tf_op | source)
XLA Modules:
  0.0 523.0 jit_solution(5357533425166158105)
XLA Ops:
  6.5 0.0 all-gather.6.cloned.1.call-start
  6.5 2.7 convert_element_type.9
  9.2 0.0 all-gather.6.cloned.1.call-update
  9.3 0.0 all-gather.8.cloned.1.call-start
  9.3 0.7 all-gather.8.cloned.1.call-update
  10.0 0.0 all-gather.10.cloned.1.call-start
  10.1 0.7 all-gather.10.cloned.1.call-update
  10.7 0.0 reduce-scatter.2.cloned.1.call-start
  10.8 77.8 %all-gather.6.cloned.1.call-done = bf16[1024,2048]{1,0:T(8,128)(2,1)} async-done(((bf16[1024,512]{1,0:T(8,128)(2,1)}), bf16[1024,2048]{1,0:T(8,128)(2,1)}) %all-gather.6.cloned.1.call-update) | async-done | bytes 4194320 | tf_op jit(solution)/shard_map/all_gather | solution.py:12
  88.6 22.7 %all-gather.8.cloned.1.call-done = bf16[1,4,2048,512]{3,2,1,0:T(8,128)(2,1)} async-done(((bf16[1,4,1024,512]{3,2,1,0:T(8,128)(2,1)}), bf16[1,4,2048,512]{3,2,1,0:T(8,128)(2,1)}) %all-gather.8.cloned.1.call-update) | async-done | bytes 8388624 | tf_op jit(solution)/shard_map/all_gather | solution.py:16
  111.3 286.4 %all-gather.10.cloned.1.call-done = bf16[1,4,1024,2048]{3,2,1,0:T(8,128)(2,1)} async-done(((bf16[1,4,1024,512]{3,2,1,0:T(8,128)(2,1)}), bf16[1,4,1024,2048]{3,2,1,0:T(8,128)(2,1)}) %all-gather.10.cloned.1.call-update) | async-done | bytes 16777232 | tf_op jit(solution)/shard_map/all_gather | solution.py:21
  397.7 29.0 %fusion.15 = f32[2048,512]{0,1:T(8,128)} fusion(bf16[1,4,1024,2048]{3,2,1,0:T(8,128)(2,1)} %all-gather.10.cloned.1.call-done, bf16[1024,2048]{1,0:T(8,128)(2,1)} %all-gather.6.cloned.1.call-done, bf16[1,4,2048,512]{3,2,1,0:T(8,128)(2,1)} %all-gather.8.cloned.1.call-done), kind=kOutput, calls=%fused_computation.7 | convolution fusion | flops 17181966336 | bytes 33554432 | tf_op jit(solution)/shard_map/pij,pil->jl/dot_general | solution.py:19
  426.7 0.0 reduce-scatter.2.cloned.1.call-update
  426.7 0.0 all-reduce.2.cloned.1.call-start
  426.8 13.4 %reduce-scatter.2.cloned.1.call-done = f32[1024,512]{0,1:T(8,128)} async-done(((f32[2048,512]{0,1:T(8,128)}), f32[1024,512]{0,1:T(8,128)}) %reduce-scatter.2.cloned.1.call-update) | async-done | bytes 2097168 | tf_op jit(solution)/shard_map/reduce_scatter | solution.py:25
  440.2 0.0 all-reduce.2.cloned.1.call-update
  440.2 73.3 %all-reduce.2.cloned.1.call-done = f32[1024,512]{0,1:T(8,128)} async-done(((f32[1024,512]{0,1:T(8,128)}), f32[1024,512]{0,1:T(8,128)}) %all-reduce.2.cloned.1.call-update) | async-done | bytes 2097168 | tf_op jit(solution)/shard_map/psum | solution.py:26
  513.6 2.9 copy.4
Async XLA Ops:
  6.5 82.0 %all-gather.6.cloned.1.call-start = ((), (), s32[]{:S(2)}) async-start(), calls=%async_computation.1 | async-start | bytes 5242880 | tf_op jit(solution)/shard_map/all_gather | solution.py:12
  9.3 102.0 %all-gather.8.cloned.1.call-start = ((), (), s32[]{:S(2)}) async-start(), calls=%async_computation.4 | async-start | bytes 12582912 | tf_op jit(solution)/shard_map/all_gather | solution.py:16
  10.0 387.7 %all-gather.10.cloned.1.call-start = ((), (), s32[]{:S(2)}) async-start(), calls=%async_computation.5 | async-start | bytes 20971520 | tf_op jit(solution)/shard_map/all_gather | solution.py:21
  10.7 429.5 %reduce-scatter.2.cloned.1.call-start = ((), (), s32[]{:S(2)}) async-start(), calls=%async_computation.2 | async-start | bytes 6291456 | tf_op jit(solution)/shard_map/reduce_scatter | solution.py:25
  426.7 86.8 %all-reduce.2.cloned.1.call-start = ((), (), s32[]{:S(2)}) async-start(), calls=%async_computation.3 | async-start | bytes 4194304 | tf_op jit(solution)/shard_map/psum | solution.py:26
Sparse Core Ops, SparseCore 0:
  9.4 79.1 all-gather.5
  90.1 21.1 all-gather.7
  112.9 284.8 all-gather.9
  426.9 13.2 reduce-scatter.1
  443.1 70.3 all-reduce.1
where the time goes:
time: 525 us; the launch traced here: 523 us
  waiting for transfers between devices  475 us (90%)
  matrix products  29 us (6%)
  between operations  13.1 us (2%)
    all_gather x1, waiting for transfers between devices, per_device(): lax.all_gather(rho_block, 'col', axis=2, tiled=True)  286 us
    all_gather x1, waiting for transfers between devices, per_device(): env_whole = lax.all_gather(env_b, 'col', axis=1, tiled=True)  77.8 us
    psum x1, waiting for transfers between devices, per_device(): env = lax.psum(row_part, 'phys')  73.3 us
    dot_general x1, matrix products, per_device(): jnp.einsum('pij,pil->jl', lax.all_gather(rho_block, 'col', axis=2, tiled=...  29 us
    all_gather x1, waiting for transfers between devices, per_device(): lax.all_gather(sigma_block, 'row', axis=1, tiled=True)  22.7 us
    reduce_scatter x1, waiting for transfers between devices, per_device(): lax.psum_scatter(partial_env, 'row', scatter_dimension=0, tiled=True)  13.4 us
  transfers between devices with their start and end apart: 5, of which 5 were waited for; matrix products, arithmetic and copies ran while one was open for 0% of the time, Pallas kernels for 0%

commit v1 on v0

v1 whole, which is shorter than its diff:
```python
import functools

import jax
import jax.numpy as jnp
from jax import lax
from jax.experimental import pallas as pl
from jax.experimental.pallas import tpu as pltpu
from jax.sharding import PartitionSpec as P

MESH = pl.DeviceIdType.MESH
NCH = 4
FROM_RIGHT = {
    0: [("r", 1, k) for k in range(4)] + [("r", 2, k) for k in range(4)],
    1: [("r", 2, 0), ("r", 2, 1), ("r", 3, 0), ("r", 3, 1), ("r", 2, 2), ("r", 3, 2), ("r", 2, 3), ("r", 3, 3)],
    2: [("r", 3, k) for k in range(4)] + [("h", p) for p in range(4)],
    3: [None] * 8,
}


def mirror(item):
    if item is None or item[0] == "h":
        return item
    return ("r", 3 - item[1], item[2])


FROM_LEFT = {3 - c: [mirror(i) for i in seq] for c, seq in FROM_RIGHT.items()}
PASS_LEFT = {
    (2, 1): [(3, 0)], (2, 2): [(3, 1), (2, 2)], (2, 3): [(3, 2), (2, 3)], (2, 4): [(3, 3)],
    (1, 1): [(2, 0)], (1, 2): [(2, 1)], (1, 5): [(2, 2)], (1, 7): [(2, 3)],
}
PASS_RIGHT = {(3 - c, t): [(3 - b, k) for b, k in v] for (c, t), v in PASS_LEFT.items()}
FIRST_LEFT = {1: [(1, k) for k in range(4)], 2: [(2, 0), (2, 1)], 3: [(3, k) for k in range(4)]}
FIRST_RIGHT = {3 - c: [(3 - b, k) for b, k in v] for c, v in FIRST_LEFT.items()}
F32 = jnp.float32
BF16 = jnp.bfloat16


def kernel(rho_ref, sig_ref, env_ref, out_ref,
           rho_g, sig, env_f, env_g, half, half_r, acc, psend, rbuf, s1, xbuf, s2, ybuf, fin,
           rl_send, rr_send, r_recv, h_send, h_recv, loc, sg_send, sg_recv,
           el_send, er_send, e_recv, ex_send, ex_recv, ey_send, ey_recv,
           row_send, row_recv, x_send, x_recv, y_send, y_recv, o_sem, z_send, z_recv):
    ph = lax.axis_index("phys")
    r = lax.axis_index("row")
    c = lax.axis_index("col")
    width = rho_g.shape[-1]
    rows = rho_g.shape[3]
    quarter = rows // 4
    ind3 = c // 3
    ind2 = c // 2 - ind3
    ind0 = (3 - c) // 3
    ind1 = 1 - ind0 - ind2 - ind3
    inds = (ind0, ind1, ind2, ind3)

    def pick(values):
        total = 0
        for i, v in zip(inds, values):
            total = total + i * v
        return total

    mate = {"row": 1 - r}
    xn = {"phys": ph + 1 - 2 * (ph % 2)}
    yn = {"phys": (ph + 2) % 4}
    left = {"col": c - 1}
    right = {"col": c + 1}

    def remote(src, dst, ss, rs, dev):
        return pltpu.make_async_remote_copy(src_ref=src, dst_ref=dst, send_sem=ss, recv_sem=rs,
                                            device_id=dev, device_id_type=MESH)

    load_env = pltpu.make_async_copy(env_ref, env_f, loc.at[0])
    load_env.start()
    load_rho = [pltpu.make_async_copy(rho_ref.at[0, :, :, pl.ds(k * width, width)], rho_g.at[c, k], loc.at[1 + k]) for k in range(NCH)]
    for cp in load_rho:
        cp.start()
    my_rows = pl.ds(pl.multiple_of(r * rows, rows), rows)
    load_sig = pltpu.make_async_copy(sig_ref.at[0], sig.at[:, my_rows, :], loc.at[1 + NCH])
    load_sig.start()

    barrier = pltpu.get_barrier_semaphore()
    for dev in (mate, xn, yn):
        pl.semaphore_signal(barrier, inc=1, device_id=dev, device_id_type=MESH)

    @pl.when(c > 0)
    def _():
        pl.semaphore_signal(barrier, inc=1, device_id=left, device_id_type=MESH)

    @pl.when(c < 3)
    def _():
        pl.semaphore_signal(barrier, inc=1, device_id=right, device_id_type=MESH)

    load_env.wait()
    env_g[c] = env_f[...].astype(BF16)
    pl.semaphore_wait(barrier, 3 + pick((1, 2, 2, 1)))

    q_rows = pl.ds(pl.multiple_of(ph * quarter, quarter), quarter)
    h_rows = pl.ds(pl.multiple_of((ph // 2) * 2 * quarter, 2 * quarter), 2 * quarter)

    def env_left(b):
        return remote(env_g.at[b, q_rows], env_g.at[b, q_rows], el_send.at[b], e_recv.at[b], left)

    def env_right(b):
        return remote(env_g.at[b, q_rows], env_g.at[b, q_rows], er_send.at[b], e_recv.at[b], right)

    def env_x(b):
        return remote(env_g.at[b, q_rows], env_g.at[b, q_rows], ex_send.at[b], ex_recv.at[b], xn)

    def env_y(b):
        return remote(env_g.at[b, h_rows], env_g.at[b, h_rows], ey_send.at[b], ey_recv.at[b], yn)

    def send_left(b, k):
        src = rho_g.at[b, k]
        return remote(src, rho_g.at[b, k], rl_send.at[b, k], r_recv.at[b, k], left)

    def send_right(b, k):
        src = rho_g.at[b, k]
        return remote(src, rho_g.at[b, k], rr_send.at[b, k], r_recv.at[b, k], right)

    @pl.when(c > 0)
    def _():
        env_left(c).start()

    @pl.when(c < 3)
    def _():
        env_right(c).start()

    give_sig = remote(sig_ref.at[0], sig.at[:, my_rows, :], sg_send, sg_recv, mate)
    give_sig.start()
    for cp in load_rho:
        cp.wait()

    def first_sends(cols_):
        for i in cols_:
            @pl.when(c == i)
            def _():
                for b, k in FIRST_LEFT.get(i, []):
                    send_left(b, k).start()
                for b, k in FIRST_RIGHT.get(i, []):
                    send_right(b, k).start()

    first_sends((0, 3))
    for d in range(1, 4):
        @pl.when(c >= d)
        def _(b=c - d):
            env_right(b).wait_recv()

            @pl.when(c < 3)
            def _():
                env_right(b).start()
            env_x(b).start()

        @pl.when(c + d <= 3)
        def _(b=c + d):
            env_left(b).wait_recv()

            @pl.when(c > 0)
            def _():
                env_left(b).start()
            env_x(b).start()
        if d == 2:
            first_sends((1, 2))

    def others(f):
        for d in range(1, 4):
            @pl.when(c >= d)
            def _(b=c - d):
                f(b)

            @pl.when(c + d <= 3)
            def _(b=c + d):
                f(b)

    def env_y_of(b):
        env_x(b).wait_recv()
        env_y(b).start()
    others(env_y_of)
    others(lambda b: env_y(b).wait_recv())
    load_sig.wait()
    give_sig.wait_recv()

    tile = min(256, rows)

    @pl.loop(0, 4)
    def _(p):
        @pl.loop(0, rows // tile)
        def _(m):
            here = pl.ds(pl.multiple_of(m * tile, tile), tile)
            total = jnp.dot(env_g[0, here, :], sig[p, pl.ds(0, 512), :], preferred_element_type=F32)
            for b in range(1, 4):
                total += jnp.dot(env_g[b, here, :], sig[p, pl.ds(b * 512, 512), :], preferred_element_type=F32)
            half[p, here, :] = total.astype(BF16)

    def unit_of(b, k):
        return (b % 2) * NCH + k

    def product(b, k, other, unit):
        acc[unit] = jnp.zeros_like(acc.at[unit])

        @pl.loop(0, 4)
        def _(p):
            acc[unit] += lax.dot_general(rho_g[b, k, p], other[p], (((0,), (0,)), ((), ())),
                                         preferred_element_type=F32)

    def row_copy(unit):
        return remote(psend.at[unit], rbuf.at[unit], row_send.at[unit], row_recv.at[unit], mate)

    def x_copy(unit):
        return remote(s1.at[unit], xbuf.at[unit], x_send.at[unit], x_recv.at[unit], xn)

    def y_copy(unit):
        return remote(s2.at[unit], ybuf.at[unit], y_send.at[unit], y_recv.at[unit], yn)

    def out_copy(unit):
        at = pl.ds(pl.multiple_of(unit * width, width), width)
        return pltpu.make_async_copy(fin.at[unit], out_ref.at[at], o_sem.at[unit])

    rem_b = pick((0, 3, 0, 0))
    mid = jnp.logical_and(c > 0, c < 3)

    def res_left(k):
        return remote(fin.at[2 * NCH + k], fin.at[NCH + k], z_send.at[k], z_recv.at[k], left)

    def res_right(k):
        return remote(fin.at[2 * NCH + k], fin.at[k], z_send.at[k], z_recv.at[k], right)

    def stage0(pos):
        valid, b, k, rem = pos

        @pl.when(valid)
        def _():
            unit = 2 * NCH + k if rem else unit_of(b, k)
            owner = b // 2
            own = 1 - (owner + r - 2 * owner * r)
            slot = own * unit + (1 - own) * (3 * NCH)
            product(b, k, half_r if rem else half, slot)

            @pl.when(b // 2 != r)
            def _():
                psend[unit] = acc[slot].astype(BF16)
                row_copy(unit).start()

    def owned(pos, f):
        valid, b, k, rem = pos

        @pl.when(jnp.logical_and(valid, b // 2 == r))
        def _():
            f(2 * NCH + k if rem else unit_of(b, k))

    def stage1(pos):
        def f(unit):
            row_copy(unit).wait_recv()
            s1[unit] = (acc[unit] + rbuf[unit].astype(F32)).astype(BF16)
            x_copy(unit).start()
        owned(pos, f)

    def stage2(pos):
        def f(unit):
            x_copy(unit).wait_recv()
            s2[unit] = (s1[unit].astype(F32) + xbuf[unit].astype(F32)).astype(BF16)
            y_copy(unit).start()
        owned(pos, f)

    def stage3(pos):
        def f(unit):
            y_copy(unit).wait_recv()
            fin[unit] = s2[unit].astype(F32) + ybuf[unit].astype(F32)
            if pos[3]:
                @pl.when(c == 1)
                def _():
                    res_left(pos[2]).start()

                @pl.when(c == 2)
                def _():
                    res_right(pos[2]).start()
            else:
                out_copy(unit).start()
        owned(pos, f)

    line = []

    def advance(pos):
        if pos is not None:
            stage0(pos)
        line.append(pos)
        n = len(line) - 1
        for lag, stage in ((2, stage1), (4, stage2), (6, stage3)):
            if n - lag >= 0 and line[n - lag] is not None:
                stage(line[n - lag])

    def half_copy(p, dev):
        return remote(half.at[p], half_r.at[p], h_send.at[p], h_recv.at[p], dev)

    true = c >= 0

    def arrive(t):
        for i in range(4):
            @pl.when(c == i)
            def _():
                for table, passed, send, wait in (
                    (FROM_RIGHT, PASS_LEFT, send_left, send_left),
                    (FROM_LEFT, PASS_RIGHT, send_right, send_right),
                ):
                    item = table[i][t - 1]
                    if item is None:
                        continue
                    if item[0] == "h":
                        half_copy(item[1], left if i == 2 else right).wait_recv()
                    else:
                        wait(item[1], item[2]).wait_recv()
                    for b, k in passed.get((i, t), []):
                        send(b, k).start()

    def positions(t):
        for table in (FROM_RIGHT, FROM_LEFT):
            items = [table[i][t - 1] for i in range(4)]
            ok = [1 if it is not None and it[0] == "r" else 0 for it in items]
            blocks = [it[1] if o else 0 for it, o in zip(items, ok)]
            chunks = [it[2] if o else 0 for it, o in zip(items, ok)]
            yield (pick(ok) == 1, pick(blocks), pick(chunks), False)

    arrive(1)
    for k in range(NCH):
        advance((true, c, k, False))

    @pl.when(c == 0)
    def _():
        for p in range(4):
            half_copy(p, right).start()

    @pl.when(c == 3)
    def _():
        for p in range(4):
            half_copy(p, left).start()
    for t in range(1, 9):
        if t > 1:
            arrive(t)
        for pos in positions(t):
            advance(pos)
    for k in range(NCH):
        advance((mid, rem_b, k, True))
    for _ in range(6):
        advance(None)

    @pl.when(jnp.logical_and(c == 0, r == 1))
    def _():
        for k in range(NCH):
            res_left(k).wait_recv()
            out_copy(NCH + k).start()

    @pl.when(jnp.logical_and(c == 3, r == 0))
    def _():
        for k in range(NCH):
            res_right(k).wait_recv()
            out_copy(k).start()

    for unit in range(2 * NCH):
        out_copy(unit).wait()
    give_sig.wait_send()

    @pl.when(c > 0)
    def _():
        env_left(c).wait_send()

    @pl.when(c < 3)
    def _():
        env_right(c).wait_send()
    for d in range(1, 4):
        @pl.when(c >= d)
        def _(b=c - d):
            @pl.when(c < 3)
            def _():
                env_right(b).wait_send()
            env_x(b).wait_send()
            env_y(b).wait_send()

        @pl.when(c + d <= 3)
        def _(b=c + d):
            @pl.when(c > 0)
            def _():
                env_left(b).wait_send()
            env_x(b).wait_send()
            env_y(b).wait_send()
    for i in range(4):
        @pl.when(c == i)
        def _():
            for first, passed, send in ((FIRST_LEFT, PASS_LEFT, send_left), (FIRST_RIGHT, PASS_RIGHT, send_right)):
                todo = list(first.get(i, []))
                for (j, t), v in passed.items():
                    if j == i:
                        todo += v
                for b, k in todo:
                    send(b, k).wait_send()
            if i in (0, 3):
                for p in range(4):
                    half_copy(p, right if i == 0 else left).wait_send()
    for pos in line:
        if pos is None:
            continue
        valid, b, k, rem = pos

        @pl.when(valid)
        def _():
            unit = 2 * NCH + k if rem else unit_of(b, k)

            @pl.when(b // 2 != r)
            def _():
                row_copy(unit).wait_send()

            @pl.when(b // 2 == r)
            def _():
                x_copy(unit).wait_send()
                y_copy(unit).wait_send()
                if rem:
                    @pl.when(c == 1)
                    def _():
                        res_left(k).wait_send()

                    @pl.when(c == 2)
                    def _():
                        res_right(k).wait_send()


def fused(rho_sites, sigma_sites, environment):
    _, pairs, rows, cols = rho_sites.shape
    width = cols // NCH
    units = 3 * NCH
    sem = pltpu.SemaphoreType.DMA
    piece = (units, width, cols)
    return pl.pallas_call(
        kernel,
        out_shape=jax.ShapeDtypeStruct(environment.shape, F32),
        in_specs=[pl.BlockSpec(memory_space=pl.ANY)] * 3,
        out_specs=pl.BlockSpec(memory_space=pl.ANY),
        scratch_shapes=[
            pltpu.VMEM((4, NCH, pairs, rows, width), BF16),
            pltpu.VMEM((pairs, 2 * rows, cols), BF16),
            pltpu.VMEM((rows, cols), F32),
            pltpu.VMEM((4, rows, cols), BF16),
            pltpu.VMEM((pairs, rows, cols), BF16),
            pltpu.VMEM((pairs, rows, cols), BF16),
            pltpu.VMEM((units + 1, width, cols), F32),
            pltpu.VMEM(piece, BF16), pltpu.VMEM(piece, BF16), pltpu.VMEM(piece, BF16),
            pltpu.VMEM(piece, BF16), pltpu.VMEM(piece, BF16), pltpu.VMEM(piece, BF16),
            pltpu.VMEM(piece, F32),
            sem((4, NCH)), sem((4, NCH)), sem((4, NCH)), sem((4,)), sem((4,)),
            sem((2 + NCH,)), sem, sem,
            sem((4,)), sem((4,)), sem((4,)), sem((4,)), sem((4,)), sem((4,)), sem((4,)),
            sem((units,)), sem((units,)), sem((units,)), sem((units,)), sem((units,)), sem((units,)),
            sem((units,)), sem((NCH,)), sem((NCH,)),
        ],
        compiler_params=pltpu.CompilerParams(
            collective_id=0, has_side_effects=True, vmem_limit_bytes=64 * 1024 * 1024 - 65536
        ),
    )(rho_sites, sigma_sites, environment)


def plain(rho_sites, sigma_sites, environment):
    env_whole = lax.all_gather(environment.astype(BF16), "col", axis=1, tiled=True)
    half = jnp.einsum(
        "ik,pkl->pil",
        env_whole,
        lax.all_gather(sigma_sites[0], "row", axis=1, tiled=True),
        preferred_element_type=F32,
    ).astype(BF16)
    partial_env = jnp.einsum(
        "pij,pil->jl",
        lax.all_gather(rho_sites[0], "col", axis=2, tiled=True),
        half,
        preferred_element_type=F32,
    )
    row_part = lax.psum_scatter(partial_env, "row", scatter_dimension=0, tiled=True)
    return lax.psum(row_part, "phys")


def solution(mesh):
    placed = (P(None, "phys", "row", "col"), P(None, "phys", "row", "col"), P("row", "col"))
    sizes = (mesh.shape["phys"], mesh.shape["row"], mesh.shape["col"])
    body = fused if sizes == (4, 2, 4) else plain
    return jax.shard_map(body, mesh=mesh, in_specs=placed, out_specs=P("row", "col"), check_vma=False)
```

time: 525 us -> 230 us (0.44)
  waiting for transfers between devices: 475 us -> 0 us
  Pallas kernels: 0 us -> 227 us
  matrix products: 29 us -> 0 us
  between operations: 13.1 us -> 0.01 us
    all_gather x3 -> x0, waiting for transfers between devices: 387 us -> none  [the longest x1 286 us: per_device(): lax.all_gather(rho_block, 'col', axis=2, tiled=True)]
    pallas_call x0 -> x1, Pallas kernels: none -> 227 us  [fused(): pl.pallas_call(kernel, out_shape=jax.ShapeDtypeStruct(environment.shape,...]
    psum x1 -> x0, waiting for transfers between devices: 73.3 us -> none  [per_device(): env = lax.psum(row_part, 'phys')]
    dot_general x1 -> x0, matrix products: 29 us -> none  [per_device(): jnp.einsum('pij,pil->jl', lax.all_gather(rho_block, 'col', axis=2, tiled=...]
    reduce_scatter x1 -> x0, waiting for transfers between devices: 13.4 us -> none  [per_device(): lax.psum_scatter(partial_env, 'row', scatter_dimension=0, tiled=True)]
  transfers between devices with their start and end apart: 5 -> 0, of which waited for: 5 -> 0; matrix products, arithmetic and copies ran while one was open for 0% -> 0% of each run, Pallas kernels for 0% -> 0%
where the time goes in v1:
time: 230 us
  Pallas kernels  227 us (99%)
  local copies, waits for them, and re-layouts  3.08 us (1%)
    pallas_call x1, Pallas kernels, fused(): pl.pallas_call(kernel, out_shape=jax.ShapeDtypeStruct(environment.shape,...  227 us

profile of v1, /device:TPU:26, one launch (start us, length us, event | category | flops | bytes accessed | tf_op | source)
XLA Modules:
  0.0 230.0 jit_solution(15126871894638186266)
XLA Ops:
  0.0 226.9 %shard_map.37 = f32[1024,512]{1,0:T(8,128)} custom-call(bf16[1,4,1024,512]{3,2,1,0:T(8,128)(2,1)} %rho_ref.1, bf16[1,4,1024,512]{3,2,1,0:T(8,128)(2,1)} %sig_ref.1, f32[1024,512]{1,0:T(8,128)} %env_ref.1), custom_call_target="tpu_custom_call" | custom-call | tf_op jit(solution)/shard_map/pallas_call | solution.py:429
  226.9 3.1 %copy.5 = f32[1024,512]{1,0:T(8,128)} copy(f32[1024,512]{1,0:T(8,128)} %shard_map.37) | data formatting | bytes 4194304

commit v2 on v1

--- a/solution.py
+++ b/solution.py
@@ -10,8 +10,8 @@
 MESH = pl.DeviceIdType.MESH
 NCH = 4
 FROM_RIGHT = {
-    0: [("r", 1, k) for k in range(4)] + [("r", 2, k) for k in range(4)],
-    1: [("r", 2, 0), ("r", 2, 1), ("r", 3, 0), ("r", 3, 1), ("r", 2, 2), ("r", 3, 2), ("r", 2, 3), ("r", 3, 3)],
+    0: [("r", 1, k) for k in range(4)] + [("r", 2, k) for k in range(3)] + [None],
+    1: [("r", 2, 0), ("r", 2, 1), ("r", 3, 0), ("r", 3, 1), ("r", 2, 2), ("r", 3, 2), ("r", 3, 3), ("r", 2, 3)],
     2: [("r", 3, k) for k in range(4)] + [("h", p) for p in range(4)],
     3: [None] * 8,
 }
@@ -25,12 +25,14 @@
 
 FROM_LEFT = {3 - c: [mirror(i) for i in seq] for c, seq in FROM_RIGHT.items()}
 PASS_LEFT = {
-    (2, 1): [(3, 0)], (2, 2): [(3, 1), (2, 2)], (2, 3): [(3, 2), (2, 3)], (2, 4): [(3, 3)],
-    (1, 1): [(2, 0)], (1, 2): [(2, 1)], (1, 5): [(2, 2)], (1, 7): [(2, 3)],
+    (2, 1): [(3, 0)], (2, 2): [(3, 1), (2, 2)], (2, 3): [(3, 2)], (2, 4): [(3, 3), (2, 3)],
+    (1, 1): [(2, 0)], (1, 2): [(2, 1)], (1, 5): [(2, 2)],
 }
 PASS_RIGHT = {(3 - c, t): [(3 - b, k) for b, k in v] for (c, t), v in PASS_LEFT.items()}
 FIRST_LEFT = {1: [(1, k) for k in range(4)], 2: [(2, 0), (2, 1)], 3: [(3, k) for k in range(4)]}
 FIRST_RIGHT = {3 - c: [(3 - b, k) for b, k in v] for c, v in FIRST_LEFT.items()}
+FOR_END = [(3, 0), (3, 1), (3, 2), (3, 3), (2, 3)]
+NREM = len(FOR_END)
 F32 = jnp.float32
 BF16 = jnp.bfloat16
 
@@ -138,7 +140,7 @@
                 for b, k in FIRST_RIGHT.get(i, []):
                     send_right(b, k).start()
 
-    first_sends((0, 3))
+    first_sends(range(4))
     for d in range(1, 4):
         @pl.when(c >= d)
         def _(b=c - d):
@@ -157,8 +159,6 @@
             def _():
                 env_left(b).start()
             env_x(b).start()
-        if d == 2:
-            first_sends((1, 2))
 
     def others(f):
         for d in range(1, 4):
@@ -193,10 +193,11 @@
     def unit_of(b, k):
         return (b % 2) * NCH + k
 
-    def product(b, k, other, unit):
-        acc[unit] = jnp.zeros_like(acc.at[unit])
-
-        @pl.loop(0, 4)
+    def product(b, k, other, unit, first=0, last=4):
+        if first == 0:
+            acc[unit] = jnp.zeros_like(acc.at[unit])
+
+        @pl.loop(first, last)
         def _(p):
             acc[unit] += lax.dot_general(rho_g[b, k, p], other[p], (((0,), (0,)), ((), ())),
                                          preferred_element_type=F32)
@@ -214,25 +215,39 @@
         at = pl.ds(pl.multiple_of(unit * width, width), width)
         return pltpu.make_async_copy(fin.at[unit], out_ref.at[at], o_sem.at[unit])
 
-    rem_b = pick((0, 3, 0, 0))
     mid = jnp.logical_and(c > 0, c < 3)
 
-    def res_left(k):
-        return remote(fin.at[2 * NCH + k], fin.at[NCH + k], z_send.at[k], z_recv.at[k], left)
-
-    def res_right(k):
-        return remote(fin.at[2 * NCH + k], fin.at[k], z_send.at[k], z_recv.at[k], right)
-
-    def stage0(pos):
-        valid, b, k, rem = pos
+    def end_chunk(q):
+        b, k = FOR_END[q]
+        return pick((0, b, 3 - b, 0)), k
+
+    def res_left(q):
+        b, k = FOR_END[q]
+        return remote(fin.at[2 * NCH + q], fin.at[(b % 2) * NCH + k], z_send.at[q], z_recv.at[q], left)
+
+    def res_right(q):
+        b, k = FOR_END[q]
+        return remote(fin.at[2 * NCH + q], fin.at[((3 - b) % 2) * NCH + k], z_send.at[q], z_recv.at[q], right)
+
+    def unit_at(pos):
+        _, b, k, q = pos
+        return unit_of(b, k) if q is None else 2 * NCH + q
+
+    def slot_at(pos):
+        _, b, k, q = pos
+        if q is not None:
+            return 2 * NCH + q
+        owner = b // 2
+        own = 1 - (owner + r - 2 * owner * r)
+        return own * unit_of(b, k) + (1 - own) * (2 * NCH + NREM)
+
+    def stage0(pos, first=0):
+        valid, b, k, q = pos
 
         @pl.when(valid)
         def _():
-            unit = 2 * NCH + k if rem else unit_of(b, k)
-            owner = b // 2
-            own = 1 - (owner + r - 2 * owner * r)
-            slot = own * unit + (1 - own) * (3 * NCH)
-            product(b, k, half_r if rem else half, slot)
+            unit, slot = unit_at(pos), slot_at(pos)
+            product(b, k, half if q is None else half_r, slot, first)
 
             @pl.when(b // 2 != r)
             def _():
@@ -240,11 +255,11 @@
                 row_copy(unit).start()
 
     def owned(pos, f):
-        valid, b, k, rem = pos
+        valid, b, k, q = pos
 
         @pl.when(jnp.logical_and(valid, b // 2 == r))
         def _():
-            f(2 * NCH + k if rem else unit_of(b, k))
+            f(unit_at(pos))
 
     def stage1(pos):
         def f(unit):
@@ -264,23 +279,23 @@
         def f(unit):
             y_copy(unit).wait_recv()
             fin[unit] = s2[unit].astype(F32) + ybuf[unit].astype(F32)
-            if pos[3]:
+            if pos[3] is not None:
                 @pl.when(c == 1)
                 def _():
-                    res_left(pos[2]).start()
+                    res_left(pos[3]).start()
 
                 @pl.when(c == 2)
                 def _():
-                    res_right(pos[2]).start()
+                    res_right(pos[3]).start()
             else:
                 out_copy(unit).start()
         owned(pos, f)
 
     line = []
 
-    def advance(pos):
+    def advance(pos, first=0):
         if pos is not None:
-            stage0(pos)
+            stage0(pos, first)
         line.append(pos)
         n = len(line) - 1
         for lag, stage in ((2, stage1), (4, stage2), (6, stage3)):
@@ -292,21 +307,18 @@
 
     true = c >= 0
 
-    def arrive(t):
+    def arrive(t, kinds="rh"):
         for i in range(4):
             @pl.when(c == i)
             def _():
-                for table, passed, send, wait in (
-                    (FROM_RIGHT, PASS_LEFT, send_left, send_left),
-                    (FROM_LEFT, PASS_RIGHT, send_right, send_right),
-                ):
+                for table, passed, send in ((FROM_RIGHT, PASS_LEFT, send_left), (FROM_LEFT, PASS_RIGHT, send_right)):
                     item = table[i][t - 1]
-                    if item is None:
+                    if item is None or item[0] not in kinds:
                         continue
                     if item[0] == "h":
                         half_copy(item[1], left if i == 2 else right).wait_recv()
                     else:
-                        wait(item[1], item[2]).wait_recv()
+                        send(item[1], item[2]).wait_recv()
                     for b, k in passed.get((i, t), []):
                         send(b, k).start()
 
@@ -316,11 +328,21 @@
             ok = [1 if it is not None and it[0] == "r" else 0 for it in items]
             blocks = [it[1] if o else 0 for it, o in zip(items, ok)]
             chunks = [it[2] if o else 0 for it, o in zip(items, ok)]
-            yield (pick(ok) == 1, pick(blocks), pick(chunks), False)
-
+            yield (pick(ok) == 1, pick(blocks), pick(chunks), None)
+
+    def for_end(q):
+        return (mid,) + end_chunk(q) + (q,)
+
+    def part_for_end(q, first, last):
+        @pl.when(mid)
+        def _():
+            product(*end_chunk(q), half_r, 2 * NCH + q, first, last)
+
+    early = {5: [(0, 0, 1), (1, 0, 1)], 6: [(0, 1, 2), (1, 1, 2), (2, 0, 2)],
+             7: [(0, 2, 3), (1, 2, 3), (2, 2, 3), (3, 0, 3)]}
     arrive(1)
     for k in range(NCH):
-        advance((true, c, k, False))
+        advance((true, c, k, None))
 
     @pl.when(c == 0)
     def _():
@@ -331,27 +353,31 @@
     def _():
         for p in range(4):
             half_copy(p, left).start()
-    for t in range(1, 9):
+
+    for t in range(1, 8):
         if t > 1:
             arrive(t)
         for pos in positions(t):
             advance(pos)
-    for k in range(NCH):
-        advance((mid, rem_b, k, True))
+        for q, first, last in early.get(t, []):
+            part_for_end(q, first, last)
+    arrive(8, "h")
+    for q in range(4):
+        advance(for_end(q), 3)
+    arrive(8, "r")
+    advance(for_end(4))
+    for pos in positions(8):
+        advance(pos)
     for _ in range(6):
         advance(None)
 
-    @pl.when(jnp.logical_and(c == 0, r == 1))
-    def _():
-        for k in range(NCH):
-            res_left(k).wait_recv()
-            out_copy(NCH + k).start()
-
-    @pl.when(jnp.logical_and(c == 3, r == 0))
-    def _():
-        for k in range(NCH):
-            res_right(k).wait_recv()
-            out_copy(k).start()
+    for i, keeper, got in ((0, 1, res_left), (3, 0, res_right)):
+        @pl.when(jnp.logical_and(c == i, r == keeper))
+        def _():
+            for q in range(NREM):
+                b, k = FOR_END[q]
+                got(q).wait_recv()
+                out_copy(unit_of(b if i == 0 else 3 - b, k)).start()
 
     for unit in range(2 * NCH):
         out_copy(unit).wait()
@@ -396,11 +422,11 @@
     for pos in line:
         if pos is None:
             continue
-        valid, b, k, rem = pos
+        valid, b, k, q = pos
 
         @pl.when(valid)
         def _():
-            unit = 2 * NCH + k if rem else unit_of(b, k)
+            unit = unit_at(pos)
 
             @pl.when(b // 2 != r)
             def _():
@@ -410,20 +436,20 @@
             def _():
                 x_copy(unit).wait_send()
                 y_copy(unit).wait_send()
-                if rem:
+                if q is not None:
                     @pl.when(c == 1)
                     def _():
-                        res_left(k).wait_send()
+                        res_left(q).wait_send()
 
                     @pl.when(c == 2)
                     def _():
-                        res_right(k).wait_send()
+                        res_right(q).wait_send()
 
 
 def fused(rho_sites, sigma_sites, environment):
     _, pairs, rows, cols = rho_sites.shape
     width = cols // NCH
-    units = 3 * NCH
+    units = 2 * NCH + NREM
     sem = pltpu.SemaphoreType.DMA
     piece = (units, width, cols)
     return pl.pallas_call(
@@ -446,7 +472,7 @@
             sem((2 + NCH,)), sem, sem,
             sem((4,)), sem((4,)), sem((4,)), sem((4,)), sem((4,)), sem((4,)), sem((4,)),
             sem((units,)), sem((units,)), sem((units,)), sem((units,)), sem((units,)), sem((units,)),
-            sem((units,)), sem((NCH,)), sem((NCH,)),
+            sem((units,)), sem((NREM,)), sem((NREM,)),
         ],
         compiler_params=pltpu.CompilerParams(
             collective_id=0, has_side_effects=True, vmem_limit_bytes=64 * 1024 * 1024 - 65536

time: 230 us -> 285 us (1.24)
  Pallas kernels: 227 us -> 282 us
    pallas_call x1, Pallas kernels: 227 us -> 282 us  [fused(): pl.pallas_call(kernel, out_shape=jax.ShapeDtypeStruct(environment.shape,...]
where the time goes in v2:
time: 285 us
  Pallas kernels  282 us (99%)
  local copies, waits for them, and re-layouts  3.08 us (1%)
    pallas_call x1, Pallas kernels, fused(): pl.pallas_call(kernel, out_shape=jax.ShapeDtypeStruct(environment.shape,...  282 us

profile of v2, /device:TPU:26, one launch (start us, length us, event | category | flops | bytes accessed | tf_op | source)
XLA Modules:
  0.0 284.6 jit_solution(18174214026284852940)
XLA Ops:
  0.0 281.5 %shard_map.37 = f32[1024,512]{1,0:T(8,128)} custom-call(bf16[1,4,1024,512]{3,2,1,0:T(8,128)(2,1)} %rho_ref.1, bf16[1,4,1024,512]{3,2,1,0:T(8,128)(2,1)} %sig_ref.1, f32[1024,512]{1,0:T(8,128)} %env_ref.1), custom_call_target="tpu_custom_call" | custom-call | tf_op jit(solution)/shard_map/pallas_call | solution.py:455
  281.5 3.1 %copy.5 = f32[1024,512]{1,0:T(8,128)} copy(f32[1024,512]{1,0:T(8,128)} %shard_map.37) | data formatting | bytes 4194304

commit v3 on v2

--- a/solution.py
+++ b/solution.py
@@ -131,16 +131,17 @@
     for cp in load_rho:
         cp.wait()
 
-    def first_sends(cols_):
+    def first_sends(cols_, first, last):
         for i in cols_:
             @pl.when(c == i)
             def _():
-                for b, k in FIRST_LEFT.get(i, []):
+                for b, k in FIRST_LEFT.get(i, [])[first:last]:
                     send_left(b, k).start()
-                for b, k in FIRST_RIGHT.get(i, []):
+                for b, k in FIRST_RIGHT.get(i, [])[first:last]:
                     send_right(b, k).start()
 
-    first_sends(range(4))
+    first_sends((0, 3), 0, 4)
+    first_sends((1, 2), 0, 1)
     for d in range(1, 4):
         @pl.when(c >= d)
         def _(b=c - d):
@@ -159,6 +160,8 @@
             def _():
                 env_left(b).start()
             env_x(b).start()
+        if d == 2:
+            first_sends((1, 2), 1, 4)
 
     def others(f):
         for d in range(1, 4):

time: 285 us -> 247 us (0.87)
  Pallas kernels: 282 us -> 243 us
    pallas_call x1, Pallas kernels: 282 us -> 243 us  [fused(): pl.pallas_call(kernel, out_shape=jax.ShapeDtypeStruct(environment.shape,...]
where the time goes in v3:
time: 247 us; the launch traced here: 246 us
  Pallas kernels  243 us (98%)
  local copies, waits for them, and re-layouts  3.08 us (1%)
    pallas_call x1, Pallas kernels, fused(): pl.pallas_call(kernel, out_shape=jax.ShapeDtypeStruct(environment.shape,...  243 us

profile of v3, /device:TPU:26, one launch (start us, length us, event | category | flops | bytes accessed | tf_op | source)
XLA Modules:
  0.0 245.8 jit_solution(1204681873669425023)
XLA Ops:
  0.0 242.7 %shard_map.37 = f32[1024,512]{1,0:T(8,128)} custom-call(bf16[1,4,1024,512]{3,2,1,0:T(8,128)(2,1)} %rho_ref.1, bf16[1,4,1024,512]{3,2,1,0:T(8,128)(2,1)} %sig_ref.1, f32[1024,512]{1,0:T(8,128)} %env_ref.1), custom_call_target="tpu_custom_call" | custom-call | tf_op jit(solution)/shard_map/pallas_call | solution.py:458
  242.7 3.1 %copy.5 = f32[1024,512]{1,0:T(8,128)} copy(f32[1024,512]{1,0:T(8,128)} %shard_map.37) | data formatting | bytes 4194304

commit v4 on v3

--- a/solution.py
+++ b/solution.py
@@ -141,7 +141,6 @@
                     send_right(b, k).start()
 
     first_sends((0, 3), 0, 4)
-    first_sends((1, 2), 0, 1)
     for d in range(1, 4):
         @pl.when(c >= d)
         def _(b=c - d):
@@ -161,7 +160,7 @@
                 env_left(b).start()
             env_x(b).start()
         if d == 2:
-            first_sends((1, 2), 1, 4)
+            first_sends((1, 2), 0, 4)
 
     def others(f):
         for d in range(1, 4):

time: 247 us -> 224 us (0.907)
  Pallas kernels: 243 us -> 220 us
    pallas_call x1, Pallas kernels: 243 us -> 220 us  [fused(): pl.pallas_call(kernel, out_shape=jax.ShapeDtypeStruct(environment.shape,...]
where the time goes in v4:
time: 224 us; the launch traced here: 223 us
  Pallas kernels  220 us (98%)
  local copies, waits for them, and re-layouts  3.08 us (1%)
    pallas_call x1, Pallas kernels, fused(): pl.pallas_call(kernel, out_shape=jax.ShapeDtypeStruct(environment.shape,...  220 us

profile of v4, /device:TPU:26, one launch (start us, length us, event | category | flops | bytes accessed | tf_op | source)
XLA Modules:
  0.0 223.4 jit_solution(1788434870216640865)
XLA Ops:
  0.0 220.3 %shard_map.37 = f32[1024,512]{1,0:T(8,128)} custom-call(bf16[1,4,1024,512]{3,2,1,0:T(8,128)(2,1)} %rho_ref.1, bf16[1,4,1024,512]{3,2,1,0:T(8,128)(2,1)} %sig_ref.1, f32[1024,512]{1,0:T(8,128)} %env_ref.1), custom_call_target="tpu_custom_call" | custom-call | tf_op jit(solution)/shard_map/pallas_call | solution.py:457
  220.4 3.1 %copy.5 = f32[1024,512]{1,0:T(8,128)} copy(f32[1024,512]{1,0:T(8,128)} %shard_map.37) | data formatting | bytes 4194304

commit v5 on v4

--- a/solution.py
+++ b/solution.py
@@ -11,7 +11,7 @@
 NCH = 4
 FROM_RIGHT = {
     0: [("r", 1, k) for k in range(4)] + [("r", 2, k) for k in range(3)] + [None],
-    1: [("r", 2, 0), ("r", 2, 1), ("r", 3, 0), ("r", 3, 1), ("r", 2, 2), ("r", 3, 2), ("r", 3, 3), ("r", 2, 3)],
+    1: [("r", 2, 0), ("r", 2, 1), ("r", 2, 2), ("r", 3, 0), ("r", 3, 1), ("r", 3, 2), ("r", 3, 3), ("r", 2, 3)],
     2: [("r", 3, k) for k in range(4)] + [("h", p) for p in range(4)],
     3: [None] * 8,
 }
@@ -25,11 +25,11 @@
 
 FROM_LEFT = {3 - c: [mirror(i) for i in seq] for c, seq in FROM_RIGHT.items()}
 PASS_LEFT = {
-    (2, 1): [(3, 0)], (2, 2): [(3, 1), (2, 2)], (2, 3): [(3, 2)], (2, 4): [(3, 3), (2, 3)],
-    (1, 1): [(2, 0)], (1, 2): [(2, 1)], (1, 5): [(2, 2)],
+    (2, 1): [(3, 0)], (2, 2): [(3, 1)], (2, 3): [(3, 2)], (2, 4): [(3, 3), (2, 3)],
+    (1, 1): [(2, 0)], (1, 2): [(2, 1)], (1, 3): [(2, 2)],
 }
 PASS_RIGHT = {(3 - c, t): [(3 - b, k) for b, k in v] for (c, t), v in PASS_LEFT.items()}
-FIRST_LEFT = {1: [(1, k) for k in range(4)], 2: [(2, 0), (2, 1)], 3: [(3, k) for k in range(4)]}
+FIRST_LEFT = {1: [(1, k) for k in range(4)], 2: [(2, 0), (2, 1), (2, 2)], 3: [(3, k) for k in range(4)]}
 FIRST_RIGHT = {3 - c: [(3 - b, k) for b, k in v] for c, v in FIRST_LEFT.items()}
 FOR_END = [(3, 0), (3, 1), (3, 2), (3, 3), (2, 3)]
 NREM = len(FOR_END)

time: 224 us -> 224 us (level)
  no operation moved by 1% of the time
where the time goes in v5:
time: 224 us; the launch traced here: 223 us
  Pallas kernels  220 us (98%)
  local copies, waits for them, and re-layouts  3.08 us (1%)
    pallas_call x1, Pallas kernels, fused(): pl.pallas_call(kernel, out_shape=jax.ShapeDtypeStruct(environment.shape,...  220 us

profile of v5, /device:TPU:26, one launch (start us, length us, event | category | flops | bytes accessed | tf_op | source)
XLA Modules:
  0.0 223.4 jit_solution(1250394317887126769)
XLA Ops:
  0.0 220.3 %shard_map.37 = f32[1024,512]{1,0:T(8,128)} custom-call(bf16[1,4,1024,512]{3,2,1,0:T(8,128)(2,1)} %rho_ref.1, bf16[1,4,1024,512]{3,2,1,0:T(8,128)(2,1)} %sig_ref.1, f32[1024,512]{1,0:T(8,128)} %env_ref.1), custom_call_target="tpu_custom_call" | custom-call | tf_op jit(solution)/shard_map/pallas_call | solution.py:457
  220.3 3.1 %copy.5 = f32[1024,512]{1,0:T(8,128)} copy(f32[1024,512]{1,0:T(8,128)} %shard_map.37) | data formatting | bytes 4194304
